TPU v7x, 32 devices: a whole 2x2x4 slice. The times are simulated.
32 devices in a mesh: freq: 2 (over y), rcv: 4 (over z), src: 4 (over x, core).
Axes of the slice: x: 2, y: 2, z: 4, core: 2. Of those that a mesh axis runs over, the one named last changes fastest.
Arguments:
- traces: float32 [256, 2, 4096], P(('freq', 'src'), None, 'rcv'), parts along dimension 0, may hold values from -6 to 6
- moveout: float32 [2, 64, 16], P(None, 'freq'), parts along dimension 1, may hold values from -0.75 to 0.75
- trace_owner: int32 [8192], P(('freq', 'rcv')), parts along dimension 0, may hold values from 0 to 3, as said below
- trace_group: int32 [8192], P(('freq', 'rcv')), parts along dimension 0, may hold values from 0 to 127
- trace_table: int32 [8192], P(('freq', 'rcv')), parts along dimension 0, may hold values from 0 to 31
- aperture: float32 [2, 16384, 8192], P(None, ('freq', 'rcv'), 'src'), parts along dimension 1, may hold values from -0.046875 to 0.046875
- shaping: float32 [256, 2, 8192], P(('freq', 'src'), None, 'rcv'), parts along dimension 0, may hold values from -0.5 to 0.5
Outputs:
- demultiple: float32 [256, 2, 8192], P(('freq', 'src'), None, 'rcv'), parts along dimension 0
There are 2 independent parts, one for each index of `freq`. A program takes and returns all parts, laid end to end along the dimension named above; each array names one. Nothing has to cross between parts.
Inputs may be any that keep to these rules, and one draw needn't show every extreme that they name: `trace_owner`: among the 1024 traces of each index of rcv (aligned blocks of the array), at most 512 name the same owner, and in every draw some owner is named by exactly 512 traces of every block.
All inputs are finite; a program needn't handle non-finite values.
Results may differ from a plain program's by a relative error of at most 0.0001.
Values sent between devices are 32-bit elements; how exact they have to be, the bound alone decides.
A program may use at most 128 MiB of HBM per device.

v0:
```python
import jax
import jax.numpy as jnp
from jax import lax
from jax.sharding import PartitionSpec as P

ITERS = 2


def from_root(value, axis, source):
    kept = jnp.where(lax.axis_index(axis) == source, value, 0).astype(value.dtype)
    return lax.psum(kept, axis)


def complex_join(partial_terms):
    return jnp.stack(
        [
            partial_terms[:, 0, 0] - partial_terms[:, 1, 1],
            partial_terms[:, 0, 1] + partial_terms[:, 1, 0],
        ],
        axis=1,
    )


def complex_product(left_side, right_side):
    real_part = left_side[:, 0] * right_side[:, 0] - left_side[:, 1] * right_side[:, 1]
    imag_part = left_side[:, 0] * right_side[:, 1] + left_side[:, 1] * right_side[:, 0]
    return jnp.stack([real_part, imag_part], axis=1)


def bin_matrix(group_code, table_code, moveout, groups, owner_mask):
    group_hot = (group_code[:, None] == jnp.arange(groups)[None, :]).astype(jnp.float32)
    group_hot = group_hot * owner_mask[:, None]
    table_hot = (table_code[:, None] == jnp.arange(moveout.shape[1])[None, :]).astype(jnp.float32)
    weights = jnp.einsum("tk,ckj->tcj", table_hot, moveout, precision=lax.Precision.HIGHEST)
    matrix = group_hot[:, None, :, None] * weights[:, :, None, :]
    return matrix.reshape(matrix.shape[0], 2, groups * moveout.shape[2])


def interpolate(values, matrix):
    return complex_join(
        jnp.einsum("sct,tdb->scdb", values, matrix, precision=lax.Precision.HIGHEST)
    )


def to_columns(panel_now):
    shots_all = lax.all_gather(panel_now, "src", axis=0, tiled=True)
    fold_count = lax.axis_size("rcv") // lax.axis_size("src")
    first_root = fold_count * lax.axis_index("src")
    pieces = [from_root(shots_all, "rcv", first_root + offset) for offset in range(fold_count)]
    return jnp.concatenate(pieces, axis=2)


def multiply(columns, aperture):
    return lax.psum_scatter(
        complex_join(
            jnp.einsum("sck,dik->scdi", columns, aperture, precision=lax.Precision.HIGHEST)
        ),
        "src",
        scatter_dimension=0,
        tiled=True,
    )


def per_device(traces, moveout, trace_owner, trace_group, trace_table, aperture, shaping):
    groups = aperture.shape[1] // moveout.shape[2]

    def one_owner(owner_index):
        owner_mask = (trace_owner == owner_index).astype(jnp.float32)
        matrix = bin_matrix(trace_group, trace_table, moveout, groups, owner_mask)
        return interpolate(traces, matrix)

    binned = lax.psum_scatter(
        lax.map(one_owner, jnp.arange(1 * lax.axis_size("rcv"), dtype=jnp.int32)),
        "rcv",
        scatter_dimension=0,
        tiled=True,
    )[0]
    panel_now = binned
    for sweep_index in range(ITERS):
        multiples = multiply(to_columns(panel_now), aperture)
        panel_now = binned - complex_product(shaping, multiples)
    return panel_now


def solution(mesh):
    in_specs = (
        P(("freq", "src"), None, "rcv"),
        P(None, "freq", None),
        P(("freq", "rcv")),
        P(("freq", "rcv")),
        P(("freq", "rcv")),
        P(None, ("freq", "rcv"), "src"),
        P(("freq", "src"), None, "rcv"),
    )
    out_specs = P(("freq", "src"), None, "rcv")
    return jax.shard_map(
        per_device, mesh=mesh, in_specs=in_specs, out_specs=out_specs, check_vma=False
    )
```

profile of v0, /device:TPU:0, one launch (start us, length us, event | category | flops | bytes accessed | tf_op | source)
XLA Modules:
  0.0 581.3 jit_solution(2520688945853668558)
XLA Ops:
  7.6 160.8 %while.10 = (s32[]{:T(128)}, f32[4,32,2,2048]{3,1,2,0:T(8,128)}, s32[1024]{0:T(1024)}, s32[4]{0:T(128)S(1)}, s32[1024]{0:T(1024)}, /*index=5*/s32[1024]{0:T(1024...) while((s32[]{:T(128)}, f32[4,32,2,2048]{3,1,2,0:T(8,128)}, s32[1024]{0:T(1024)}, s32[4]{0:T(128)S(1)}, ...), condition=%wide.region_1.2_spmd, body=%wide.region_0.1_spmd.sunk | while | flops 3238561792 | bytes 55632548 | solution.py:73
  8.2 1.3 compare_convert_fusion.2
  10.3 4.3 mul.92
  14.8 12.2 %bitcast_multiply_fusion.2 = f32[1024,2,2048]{0,2,1:T(8,128)} fusion(f32[1024,2,16]{0,2,1:T(8,128)S(1)} %bitcast.96, f32[1024,2048]{0,1:T(8,128)} %bitcast.95), kind=kLoop, calls=%fused_computation.2.clone.1 | loop fusion | flops 4194304 | bytes 25296896 | tf_op jit(solution)/shard_map/while/body/eval_jaxpr/mul | solution.py:35
  27.1 19.8 %fusion.39 = f32[32,2,2,2048]{3,0,1,2:T(8,128)S(1)} fusion(f32[1024,2,2048]{0,2,1:T(8,128)} %bitcast_multiply_fusion.2, f32[32,2,1024]{2,0,1:T(8,128)S(1)} %get-tuple-element.164), kind=kOutput, calls=%fused_computation.3.clone.1 | convolution fusion | flops 3221225472 | bytes 18087936 | tf_op jit(solution)/shard_map/while/body/eval_jaxpr/sct,tdb->scdb/dot_general | solution.py:41
  48.4 1.3 compare_convert_fusion.2
  50.5 4.3 mul.92
  55.0 12.2 %bitcast_multiply_fusion.2 = f32[1024,2,2048]{0,2,1:T(8,128)} fusion(f32[1024,2,16]{0,2,1:T(8,128)S(1)} %bitcast.96, f32[1024,2048]{0,1:T(8,128)} %bitcast.95), kind=kLoop, calls=%fused_computation.2.clone.1 | loop fusion | flops 4194304 | bytes 25296896 | tf_op jit(solution)/shard_map/while/body/eval_jaxpr/mul | solution.py:35
  67.3 19.8 %fusion.39 = f32[32,2,2,2048]{3,0,1,2:T(8,128)S(1)} fusion(f32[1024,2,2048]{0,2,1:T(8,128)} %bitcast_multiply_fusion.2, f32[32,2,1024]{2,0,1:T(8,128)S(1)} %get-tuple-element.164), kind=kOutput, calls=%fused_computation.3.clone.1 | convolution fusion | flops 3221225472 | bytes 18087936 | tf_op jit(solution)/shard_map/while/body/eval_jaxpr/sct,tdb->scdb/dot_general | solution.py:41
  88.6 1.3 compare_convert_fusion.2
  90.7 4.3 mul.92
  95.2 12.2 %bitcast_multiply_fusion.2 = f32[1024,2,2048]{0,2,1:T(8,128)} fusion(f32[1024,2,16]{0,2,1:T(8,128)S(1)} %bitcast.96, f32[1024,2048]{0,1:T(8,128)} %bitcast.95), kind=kLoop, calls=%fused_computation.2.clone.1 | loop fusion | flops 4194304 | bytes 25296896 | tf_op jit(solution)/shard_map/while/body/eval_jaxpr/mul | solution.py:35
  107.5 19.8 %fusion.39 = f32[32,2,2,2048]{3,0,1,2:T(8,128)S(1)} fusion(f32[1024,2,2048]{0,2,1:T(8,128)} %bitcast_multiply_fusion.2, f32[32,2,1024]{2,0,1:T(8,128)S(1)} %get-tuple-element.164), kind=kOutput, calls=%fused_computation.3.clone.1 | convolution fusion | flops 3221225472 | bytes 18087936 | tf_op jit(solution)/shard_map/while/body/eval_jaxpr/sct,tdb->scdb/dot_general | solution.py:41
  128.8 1.3 compare_convert_fusion.2
  130.9 4.3 mul.92
  135.4 12.2 %bitcast_multiply_fusion.2 = f32[1024,2,2048]{0,2,1:T(8,128)} fusion(f32[1024,2,16]{0,2,1:T(8,128)S(1)} %bitcast.96, f32[1024,2048]{0,1:T(8,128)} %bitcast.95), kind=kLoop, calls=%fused_computation.2.clone.1 | loop fusion | flops 4194304 | bytes 25296896 | tf_op jit(solution)/shard_map/while/body/eval_jaxpr/mul | solution.py:35
  147.6 19.8 %fusion.39 = f32[32,2,2,2048]{3,0,1,2:T(8,128)S(1)} fusion(f32[1024,2,2048]{0,2,1:T(8,128)} %bitcast_multiply_fusion.2, f32[32,2,1024]{2,0,1:T(8,128)S(1)} %get-tuple-element.164), kind=kOutput, calls=%fused_computation.3.clone.1 | convolution fusion | flops 3221225472 | bytes 18087936 | tf_op jit(solution)/shard_map/while/body/eval_jaxpr/sct,tdb->scdb/dot_general | solution.py:41
  168.5 46.5 %reduce-scatter.4.cloned.1.call-done = f32[1,32,2,2048]{3,1,2,0:T(8,128)} async-done(((f32[4,32,2,2048]{3,1,2,0:T(8,128)}), f32[1,32,2,2048]{3,1,2,0:T(8,128)}) %reduce-scatter.4.cloned.1.call-update) | async-done | bytes 524304 | tf_op jit(solution)/shard_map/reduce_scatter | solution.py:72
  215.0 23.3 %all-gather.6.cloned.1.call-done = f32[1,128,2,2048]{3,1,2,0:T(8,128)} async-done(((f32[1,32,2,2048]{3,1,2,0:T(8,128)}), f32[1,128,2,2048]{3,1,2,0:T(8,128)}) %all-gather.6.cloned.1.call-update) | async-done | bytes 2097168 | tf_op jit(solution)/shard_map/all_gather | solution.py:46
  238.3 3.1 select_bitcast_fusion
  241.7 85.9 %all-reduce.3.cloned.1.call-done = f32[128,2,2048]{2,0,1:T(8,128)} async-done(((f32[128,2,2048]{2,0,1:T(8,128)}), f32[128,2,2048]{2,0,1:T(8,128)}) %all-reduce.3.cloned.1.call-update) | async-done | bytes 2097168 | tf_op jit(solution)/shard_map/psum | solution.py:11
  327.6 33.0 %fusion.15 = f32[128,2,2,2048]{3,0,2,1:T(8,128)S(1)} fusion(f32[2,2048,2048]{2,1,0:T(8,128)} %param.14, f32[128,2,2048]{2,0,1:T(8,128)} %all-reduce.3.cloned.1.call-done), kind=kOutput, calls=%fused_computation.21 | convolution fusion | flops 25769803776 | bytes 39845888 | tf_op jit(solution)/shard_map/sck,dik->scdi/dot_general | solution.py:56
  360.9 1.5 pad_maximum_fusion
  363.8 28.9 %reduce-scatter.6.cloned.1.call-done = f32[32,2,2048]{2,0,1:T(8,128)} async-done(((f32[128,2,2048]{2,0,1:T(8,128)}), f32[32,2,2048]{2,0,1:T(8,128)}) %reduce-scatter.6.cloned.1.call-update) | async-done | bytes 524304 | tf_op jit(solution)/shard_map/reduce_scatter | solution.py:54
  392.7 1.2 multiply_subtract_fusion.1
  394.9 22.7 %all-gather.4.cloned.1.call-done = f32[128,2,2048]{2,0,1:T(8,128)} async-done(((f32[32,2,2048]{2,0,1:T(8,128)}), f32[128,2,2048]{2,0,1:T(8,128)}) %all-gather.4.cloned.1.call-update) | async-done | bytes 2097168 | tf_op jit(solution)/shard_map/all_gather | solution.py:46
  417.6 3.1 broadcast_select_fusion
  421.0 85.9 %all-reduce.5.cloned.1.call-done = f32[128,2,2048]{2,0,1:T(8,128)} async-done(((f32[128,2,2048]{2,0,1:T(8,128)}), f32[128,2,2048]{2,0,1:T(8,128)}) %all-reduce.5.cloned.1.call-update) | async-done | bytes 2097168 | tf_op jit(solution)/shard_map/psum | solution.py:11
  506.9 33.0 %fusion.13 = f32[128,2,2,2048]{3,0,2,1:T(8,128)S(1)} fusion(f32[2,2048,2048]{2,1,0:T(8,128)} %param.14, f32[128,2,2048]{2,0,1:T(8,128)} %all-reduce.5.cloned.1.call-done), kind=kOutput, calls=%fused_computation.19 | convolution fusion | flops 25769803776 | bytes 39845888 | tf_op jit(solution)/shard_map/sck,dik->scdi/dot_general | solution.py:56
  540.1 1.5 pad_maximum_fusion.1
  541.6 30.3 %reduce-scatter.8.cloned.1.call-done = f32[32,2,2048]{2,0,1:T(8,128)} async-done(((f32[128,2,2048]{2,0,1:T(8,128)}), f32[32,2,2048]{2,0,1:T(8,128)}) %reduce-scatter.8.cloned.1.call-update) | async-done | bytes 524304 | tf_op jit(solution)/shard_map/reduce_scatter | solution.py:54
  572.0 1.2 multiply_subtract_fusion
  (67 shorter events, 15.7 us)
Async XLA Ops:
  6.5 208.4 %reduce-scatter.4.cloned.1.call-start = ((), (), s32[]{:S(2)}) async-start(), calls=%async_computation.3 | async-start | bytes 2621440 | tf_op jit(solution)/shard_map/reduce_scatter | solution.py:72
  10.3 4.4 copy-start.2
  10.3 4.3 copy-start.3
  50.5 4.4 copy-start.2
  50.5 4.3 copy-start.3
  90.7 4.4 copy-start.2
  90.7 4.3 copy-start.3
  130.9 4.4 copy-start.2
  130.9 4.3 copy-start.3
  168.4 69.9 %all-gather.6.cloned.1.call-start = ((), (), s32[]{:S(2)}) async-start(), calls=%async_computation.9 | async-start | bytes 2621440 | tf_op jit(solution)/shard_map/all_gather | solution.py:46
  214.9 112.7 %all-reduce.3.cloned.1.call-start = ((), (), s32[]{:S(2)}) async-start(), calls=%async_computation.4 | async-start | bytes 4194304 | tf_op jit(solution)/shard_map/psum | solution.py:11
  241.4 151.2 %reduce-scatter.6.cloned.1.call-start = ((), (), s32[]{:S(2)}) async-start(), calls=%async_computation.5 | async-start | bytes 2621440 | tf_op jit(solution)/shard_map/reduce_scatter | solution.py:54
  362.3 1.0 copy-start.1
  362.3 31.6 %copy-start = (f32[1,32,2,2048]{3,1,2,0:T(8,128)S(1)}, f32[1,32,2,2048]{3,1,2,0:T(8,128)}, u32[]{:S(2)}) copy-start(f32[1,32,2,2048]{3,1,2,0:T(8,128)} %reduce-scatter.4.cloned.1.call-done) | copy-start | bytes 1572868
  362.4 55.2 %all-gather.4.cloned.1.call-start = ((), (), s32[]{:S(2)}) async-start(), calls=%async_computation.6 | async-start | bytes 2621440 | tf_op jit(solution)/shard_map/all_gather | solution.py:46
  394.8 112.1 %all-reduce.5.cloned.1.call-start = ((), (), s32[]{:S(2)}) async-start(), calls=%async_computation.7 | async-start | bytes 4194304 | tf_op jit(solution)/shard_map/psum | solution.py:11
  420.7 151.2 %reduce-scatter.8.cloned.1.call-start = ((), (), s32[]{:S(2)}) async-start(), calls=%async_computation.8 | async-start | bytes 2621440 | tf_op jit(solution)/shard_map/reduce_scatter | solution.py:54
Sparse Core Ops, SparseCore 0:
  168.5 46.3 reduce-scatter.3
  216.5 21.7 all-gather.5
  241.6 86.0 all-reduce.2
  362.5 30.1 reduce-scatter.5
  394.9 22.5 all-gather.3
  420.8 86.0 all-reduce.4
  541.8 30.1 reduce-scatter.7
where the time goes:
time: 582 us; the launch traced here: 581 us
  waiting for transfers between devices  324 us (56%)
  matrix products  146 us (25%)
  other arithmetic  73.9 us (13%)
  local copies, waits for them, and re-layouts  23.4 us (4%)
  between operations  13.6 us (2%)
    psum x2, waiting for transfers between devices, from_root(): return lax.psum(kept, axis)  172 us
    dot_general x4, matrix products, interpolate(): jnp.einsum('sct,tdb->scdb', values, matrix, precision=lax.Precision.HIGHEST)  79.2 us
    dot_general x2, matrix products, multiply(): jnp.einsum('sck,dik->scdi', columns, aperture, precision=lax.Precision.HI...  66 us
    reduce_scatter x2, waiting for transfers between devices, multiply(): lax.psum_scatter(complex_join(jnp.einsum('sck,dik->scdi', columns, apertu...  59.2 us
    mul x4, other arithmetic, bin_matrix(): matrix = group_hot[:, None, :, None] * weights[:, :, None, :]  48.9 us
    reduce_scatter x1, waiting for transfers between devices, per_device(): lax.psum_scatter(lax.map(one_owner, jnp.arange(1 * lax.axis_size('rcv'),...  46.5 us
    all_gather x2, waiting for transfers between devices, to_columns(): shots_all = lax.all_gather(panel_now, 'src', axis=0, tiled=True)  46 us
    mul x4, local copies, waits for them, and re-layouts, bin_matrix(): matrix = group_hot[:, None, :, None] * weights[:, :, None, :]  17.3 us
  transfers between devices with their start and end apart: 7, of which 7 were waited for; matrix products, arithmetic and copies ran while one was open for 0% of the time, Pallas kernels for 0%

commit v1 on v0

--- a/solution.py
+++ b/solution.py
@@ -43,7 +43,14 @@
 
 
 def to_columns(panel_now):
-    shots_all = lax.all_gather(panel_now, "src", axis=0, tiled=True)
+    ways, here, step = (lax.axis_size("src"), lax.axis_index("src"), panel_now.shape[0])
+    line, have = (panel_now, 1)
+    while have < ways:
+        line = jnp.concatenate(
+            [line, lax.ppermute(line, "src", [(d, (d - have) % ways) for d in range(ways)])], axis=0
+        )
+        have = 2 * have
+    shots_all = jnp.roll(line, here * step, axis=0)
     fold_count = lax.axis_size("rcv") // lax.axis_size("src")
     first_root = fold_count * lax.axis_index("src")
     pieces = [from_root(shots_all, "rcv", first_root + offset) for offset in range(fold_count)]

time: 582 us -> 601 us (1.033)
  waiting for transfers between devices: 324 us -> 341 us
    ppermute x0 -> x4, waiting for transfers between devices: none -> 62.6 us  [to_columns(): lax.ppermute(line, 'src', [(d, (d - have) % ways) for d in range(ways)])]
    all_gather x2 -> x0, waiting for transfers between devices: 46 us -> none  [to_columns(): shots_all = lax.all_gather(panel_now, 'src', axis=0, tiled=True)]
  transfers between devices with their start and end apart: 7 -> 9, of which waited for: 7 -> 9; matrix products, arithmetic and copies ran while one was open for 0% -> 0% of each run, Pallas kernels for 0% -> 0%
where the time goes in v1:
time: 601 us; the launch traced here: 600 us
  waiting for transfers between devices  341 us (57%)
  matrix products  146 us (24%)
  other arithmetic  73.5 us (12%)
  local copies, waits for them, and re-layouts  23.4 us (4%)
  between operations  13.2 us (2%)
    psum x2, waiting for transfers between devices, from_root(): return lax.psum(kept, axis)  172 us
    dot_general x4, matrix products, interpolate(): jnp.einsum('sct,tdb->scdb', values, matrix, precision=lax.Precision.HIGHEST)  79.2 us
    dot_general x2, matrix products, multiply(): jnp.einsum('sck,dik->scdi', columns, aperture, precision=lax.Precision.HI...  65.8 us
    ppermute x4, waiting for transfers between devices, to_columns(): lax.ppermute(line, 'src', [(d, (d - have) % ways) for d in range(ways)])  62.6 us
    reduce_scatter x2, waiting for transfers between devices, multiply(): lax.psum_scatter(complex_join(jnp.einsum('sck,dik->scdi', columns, apertu...  59.3 us
    mul x4, other arithmetic, bin_matrix(): matrix = group_hot[:, None, :, None] * weights[:, :, None, :]  49 us
    reduce_scatter x1, waiting for transfers between devices, per_device(): lax.psum_scatter(lax.map(one_owner, jnp.arange(1 * lax.axis_size('rcv'),...  46.5 us
    mul x4, local copies, waits for them, and re-layouts, bin_matrix(): matrix = group_hot[:, None, :, None] * weights[:, :, None, :]  17.3 us
  transfers between devices with their start and end apart: 9, of which 9 were waited for; matrix products, arithmetic and copies ran while one was open for 0% of the time, Pallas kernels for 0%

profile of v1, /device:TPU:0, one launch (start us, length us, event | category | flops | bytes accessed | tf_op | source)
XLA Modules:
  0.0 600.3 jit_solution(11342434491342964950)
XLA Ops:
  7.6 160.9 %while.10 = (s32[]{:T(128)}, f32[4,32,2,2048]{3,1,2,0:T(8,128)}, s32[1024]{0:T(1024)}, s32[4]{0:T(128)S(1)}, s32[1024]{0:T(1024)}, /*index=5*/s32[1024]{0:T(1024...) while((s32[]{:T(128)}, f32[4,32,2,2048]{3,1,2,0:T(8,128)}, s32[1024]{0:T(1024)}, s32[4]{0:T(128)S(1)}, ...), condition=%wide.region_1.2_spmd, body=%wide.region_0.1_spmd.sunk | while | flops 3238561792 | bytes 55632548 | solution.py:80
  10.3 4.3 mul.97
  14.8 12.3 %bitcast_multiply_fusion.2 = f32[1024,2,2048]{0,2,1:T(8,128)} fusion(f32[1024,2,16]{0,2,1:T(8,128)S(1)} %bitcast.94, f32[1024,2048]{0,1:T(8,128)} %bitcast.93), kind=kLoop, calls=%fused_computation.2.clone.1 | loop fusion | flops 4194304 | bytes 25296896 | tf_op jit(solution)/shard_map/while/body/eval_jaxpr/mul | solution.py:35
  27.1 19.8 %fusion.51 = f32[32,2,2,2048]{3,0,1,2:T(8,128)S(1)} fusion(f32[1024,2,2048]{0,2,1:T(8,128)} %bitcast_multiply_fusion.2, f32[32,2,1024]{2,0,1:T(8,128)S(1)} %get-tuple-element.165), kind=kOutput, calls=%fused_computation.3.clone.1 | convolution fusion | flops 3221225472 | bytes 18087936 | tf_op jit(solution)/shard_map/while/body/eval_jaxpr/sct,tdb->scdb/dot_general | solution.py:41
  48.4 1.3 compare_convert_fusion.2
  50.5 4.3 mul.97
  55.1 12.3 %bitcast_multiply_fusion.2 = f32[1024,2,2048]{0,2,1:T(8,128)} fusion(f32[1024,2,16]{0,2,1:T(8,128)S(1)} %bitcast.94, f32[1024,2048]{0,1:T(8,128)} %bitcast.93), kind=kLoop, calls=%fused_computation.2.clone.1 | loop fusion | flops 4194304 | bytes 25296896 | tf_op jit(solution)/shard_map/while/body/eval_jaxpr/mul | solution.py:35
  67.3 19.8 %fusion.51 = f32[32,2,2,2048]{3,0,1,2:T(8,128)S(1)} fusion(f32[1024,2,2048]{0,2,1:T(8,128)} %bitcast_multiply_fusion.2, f32[32,2,1024]{2,0,1:T(8,128)S(1)} %get-tuple-element.165), kind=kOutput, calls=%fused_computation.3.clone.1 | convolution fusion | flops 3221225472 | bytes 18087936 | tf_op jit(solution)/shard_map/while/body/eval_jaxpr/sct,tdb->scdb/dot_general | solution.py:41
  88.7 1.3 compare_convert_fusion.2
  90.8 4.3 mul.97
  95.3 12.3 %bitcast_multiply_fusion.2 = f32[1024,2,2048]{0,2,1:T(8,128)} fusion(f32[1024,2,16]{0,2,1:T(8,128)S(1)} %bitcast.94, f32[1024,2048]{0,1:T(8,128)} %bitcast.93), kind=kLoop, calls=%fused_computation.2.clone.1 | loop fusion | flops 4194304 | bytes 25296896 | tf_op jit(solution)/shard_map/while/body/eval_jaxpr/mul | solution.py:35
  107.5 19.8 %fusion.51 = f32[32,2,2,2048]{3,0,1,2:T(8,128)S(1)} fusion(f32[1024,2,2048]{0,2,1:T(8,128)} %bitcast_multiply_fusion.2, f32[32,2,1024]{2,0,1:T(8,128)S(1)} %get-tuple-element.165), kind=kOutput, calls=%fused_computation.3.clone.1 | convolution fusion | flops 3221225472 | bytes 18087936 | tf_op jit(solution)/shard_map/while/body/eval_jaxpr/sct,tdb->scdb/dot_general | solution.py:41
  128.9 1.3 compare_convert_fusion.2
  131.0 4.3 mul.97
  135.5 12.3 %bitcast_multiply_fusion.2 = f32[1024,2,2048]{0,2,1:T(8,128)} fusion(f32[1024,2,16]{0,2,1:T(8,128)S(1)} %bitcast.94, f32[1024,2048]{0,1:T(8,128)} %bitcast.93), kind=kLoop, calls=%fused_computation.2.clone.1 | loop fusion | flops 4194304 | bytes 25296896 | tf_op jit(solution)/shard_map/while/body/eval_jaxpr/mul | solution.py:35
  147.8 19.8 %fusion.51 = f32[32,2,2,2048]{3,0,1,2:T(8,128)S(1)} fusion(f32[1024,2,2048]{0,2,1:T(8,128)} %bitcast_multiply_fusion.2, f32[32,2,1024]{2,0,1:T(8,128)S(1)} %get-tuple-element.165), kind=kOutput, calls=%fused_computation.3.clone.1 | convolution fusion | flops 3221225472 | bytes 18087936 | tf_op jit(solution)/shard_map/while/body/eval_jaxpr/sct,tdb->scdb/dot_general | solution.py:41
  168.6 46.5 %reduce-scatter.4.cloned.1.call-done = f32[1,32,2,2048]{3,1,2,0:T(8,128)} async-done(((f32[4,32,2,2048]{3,1,2,0:T(8,128)}), f32[1,32,2,2048]{3,1,2,0:T(8,128)}) %reduce-scatter.4.cloned.1.call-update) | async-done | bytes 524304 | tf_op jit(solution)/shard_map/reduce_scatter | solution.py:79
  215.5 7.0 %collective-permute-done = f32[32,2,2048]{2,0,1:T(8,128)S(1)} collective-permute-done((f32[32,2,2048]{2,0,1:T(8,128)}, f32[32,2,2048]{2,0,1:T(8,128)S(1)}, u32[]{:S(2)}, u32[]{:S(2)}) %collective-permute-start) | collective-permute-done | bytes 524320 | tf_op jit(solution)/shard_map/ppermute | solution.py:50
  224.8 24.7 %collective-permute-done.1 = f32[64,2,2048]{2,0,1:T(8,128)S(1)} collective-permute-done((f32[64,2,2048]{2,0,1:T(8,128)S(1)}, f32[64,2,2048]{2,0,1:T(8,128)S(1)}, u32[]{:S(2)}, u32[]{:S(2)}) %collective-permute-start.1) | collective-permute-done | bytes 1048608 | tf_op jit(solution)/shard_map/ppermute | solution.py:50
  249.5 2.7 fusion.26
  252.4 84.9 %all-reduce.3.cloned.1.call-done = f32[128,2,2048]{2,0,1:T(8,128)} async-done(((f32[128,2,2048]{2,0,1:T(8,128)}), f32[128,2,2048]{2,0,1:T(8,128)}) %all-reduce.3.cloned.1.call-update) | async-done | bytes 2097168 | tf_op jit(solution)/shard_map/psum | solution.py:11
  337.3 32.9 %fusion.15 = f32[128,2,2,2048]{3,0,2,1:T(8,128)S(1)} fusion(f32[2,2048,2048]{2,1,0:T(8,128)} %param.16, f32[128,2,2048]{2,0,1:T(8,128)} %all-reduce.3.cloned.1.call-done), kind=kOutput, calls=%fused_computation.21 | convolution fusion | flops 25769803776 | bytes 39845888 | tf_op jit(solution)/shard_map/sck,dik->scdi/dot_general | solution.py:63
  370.5 1.5 pad_maximum_fusion
  373.4 28.9 %reduce-scatter.6.cloned.1.call-done = f32[32,2,2048]{2,0,1:T(8,128)} async-done(((f32[128,2,2048]{2,0,1:T(8,128)}), f32[32,2,2048]{2,0,1:T(8,128)}) %reduce-scatter.6.cloned.1.call-update) | async-done | bytes 524304 | tf_op jit(solution)/shard_map/reduce_scatter | solution.py:61
  403.7 6.7 %collective-permute-done.2 = f32[32,2,2048]{2,0,1:T(8,128)S(1)} collective-permute-done((f32[32,2,2048]{2,0,1:T(8,128)S(1)}, f32[32,2,2048]{2,0,1:T(8,128)S(1)}, u32[]{:S(2)}, u32[]{:S(2)}) %collective-permute-start.2) | collective-permute-done | bytes 524320 | tf_op jit(solution)/shard_map/ppermute | solution.py:50
  410.5 1.4 collective-permute-start.3
  411.8 24.1 %collective-permute-done.3 = f32[64,2,2048]{2,0,1:T(8,128)S(1)} collective-permute-done((f32[64,2,2048]{2,0,1:T(8,128)S(1)}, f32[64,2,2048]{2,0,1:T(8,128)S(1)}, u32[]{:S(2)}, u32[]{:S(2)}) %collective-permute-start.3) | collective-permute-done | bytes 1048608 | tf_op jit(solution)/shard_map/ppermute | solution.py:50
  436.0 2.7 fusion.20
  438.9 87.3 %all-reduce.5.cloned.1.call-done = f32[128,2,2048]{2,0,1:T(8,128)} async-done(((f32[128,2,2048]{2,0,1:T(8,128)}), f32[128,2,2048]{2,0,1:T(8,128)}) %all-reduce.5.cloned.1.call-update) | async-done | bytes 2097168 | tf_op jit(solution)/shard_map/psum | solution.py:11
  526.2 32.9 %fusion.13 = f32[128,2,2,2048]{3,0,2,1:T(8,128)S(1)} fusion(f32[2,2048,2048]{2,1,0:T(8,128)} %param.16, f32[128,2,2048]{2,0,1:T(8,128)} %all-reduce.5.cloned.1.call-done), kind=kOutput, calls=%fused_computation.19 | convolution fusion | flops 25769803776 | bytes 39845888 | tf_op jit(solution)/shard_map/sck,dik->scdi/dot_general | solution.py:63
  559.4 1.5 pad_maximum_fusion.1
  560.9 30.3 %reduce-scatter.8.cloned.1.call-done = f32[32,2,2048]{2,0,1:T(8,128)} async-done(((f32[128,2,2048]{2,0,1:T(8,128)}), f32[32,2,2048]{2,0,1:T(8,128)}) %reduce-scatter.8.cloned.1.call-update) | async-done | bytes 524304 | tf_op jit(solution)/shard_map/reduce_scatter | solution.py:61
  (71 shorter events, 21.5 us)
Async XLA Ops:
  6.5 208.5 %reduce-scatter.4.cloned.1.call-start = ((), (), s32[]{:S(2)}) async-start(), calls=%async_computation.3 | async-start | bytes 2621440 | tf_op jit(solution)/shard_map/reduce_scatter | solution.py:79
  10.3 4.3 copy-start.2
  10.3 4.3 copy-start.3
  50.5 4.3 copy-start.2
  50.5 4.3 copy-start.3
  90.7 4.3 copy-start.2
  90.8 4.3 copy-start.3
  131.0 4.3 copy-start.2
  131.0 4.3 copy-start.3
  168.5 168.8 %all-reduce.3.cloned.1.call-start = ((), (), s32[]{:S(2)}) async-start(), calls=%async_computation.4 | async-start | bytes 4194304 | tf_op jit(solution)/shard_map/psum | solution.py:11
  215.0 34.5 %copy-start = (f32[1,32,2,2048]{3,1,2,0:T(8,128)S(1)}, f32[1,32,2,2048]{3,1,2,0:T(8,128)}, u32[]{:S(2)}) copy-start(f32[1,32,2,2048]{3,1,2,0:T(8,128)} %reduce-scatter.4.cloned.1.call-done) | copy-start | bytes 1572868
  215.0 7.5 %collective-permute-start = (f32[32,2,2048]{2,0,1:T(8,128)}, f32[32,2,2048]{2,0,1:T(8,128)S(1)}, u32[]{:S(2)}, u32[]{:S(2)}) collective-permute-start(f32[32,2,2048]{2,0,1:T(8,128)} %bitcast.95), channel_id=1, source_target_pairs={{0,3},{1,0},{2,1},{3,2},{4,7},{5,4},{6,5},{7,6},{8,11},{9,8},{10,9... | collective-permute-start | bytes 1572872 | tf_op jit(solution)/shard_map/ppermute | solution.py:50
  223.7 25.8 %collective-permute-start.1 = (f32[64,2,2048]{2,0,1:T(8,128)S(1)}, f32[64,2,2048]{2,0,1:T(8,128)S(1)}, u32[]{:S(2)}, u32[]{:S(2)}) collective-permute-start(f32[64,2,2048]{2,0,1:T(8,128)S(1)} %pad_maximum_fusion.2), channel_id=1, source_target_pairs={{0,2},{1,3},{2,0},{3,1},{4,6},{5,7},{6,4},{7,5},{8,10},{9,11},{10,... | collective-permute-start | bytes 3145736 | tf_op jit(solution)/shard_map/ppermute | solution.py:50
  252.2 150.1 %reduce-scatter.6.cloned.1.call-start = ((), (), s32[]{:S(2)}) async-start(), calls=%async_computation.5 | async-start | bytes 2621440 | tf_op jit(solution)/shard_map/reduce_scatter | solution.py:61
  372.0 1.0 copy-start.1
  372.0 154.2 %all-reduce.5.cloned.1.call-start = ((), (), s32[]{:S(2)}) async-start(), calls=%async_computation.6 | async-start | bytes 4194304 | tf_op jit(solution)/shard_map/psum | solution.py:11
  403.6 6.8 %collective-permute-start.2 = (f32[32,2,2048]{2,0,1:T(8,128)S(1)}, f32[32,2,2048]{2,0,1:T(8,128)S(1)}, u32[]{:S(2)}, u32[]{:S(2)}) collective-permute-start(f32[32,2,2048]{2,0,1:T(8,128)S(1)} %maximum_subtract_fusion), channel_id=1, source_target_pairs={{0,3},{1,0},{2,1},{3,2},{4,7},{5,4},{6,5},{7,6},{8,11},{9,8},{10,9... | collective-permute-start | bytes 1572872 | tf_op jit(solution)/shard_map/ppermute | solution.py:50
  410.5 25.5 %collective-permute-start.3 = (f32[64,2,2048]{2,0,1:T(8,128)S(1)}, f32[64,2,2048]{2,0,1:T(8,128)S(1)}, u32[]{:S(2)}, u32[]{:S(2)}) collective-permute-start(f32[64,2,2048]{2,0,1:T(8,128)S(1)} %pad_maximum_fusion.3), channel_id=1, source_target_pairs={{0,2},{1,3},{2,0},{3,1},{4,6},{5,7},{6,4},{7,5},{8,10},{9,11},{10,... | collective-permute-start | bytes 3145736 | tf_op jit(solution)/shard_map/ppermute | solution.py:50
  438.6 152.6 %reduce-scatter.8.cloned.1.call-start = ((), (), s32[]{:S(2)}) async-start(), calls=%async_computation.7 | async-start | bytes 2621440 | tf_op jit(solution)/shard_map/reduce_scatter | solution.py:61
Sparse Core Ops, SparseCore 0:
  168.6 46.3 reduce-scatter.3
  252.3 84.9 all-reduce.2
  372.1 30.1 reduce-scatter.5
  438.8 87.4 all-reduce.4
  561.1 30.1 reduce-scatter.7
